TPU v7x, 32 devices: a whole 2x2x4 slice. The times are simulated.
32 devices in a mesh: dp: 16 (over z, y, x), seq: 2 (over core).
Axes of the slice: x: 2, y: 2, z: 4, core: 2. Of those that a mesh axis runs over, the one named last changes fastest.
Arguments:
- tokens: bfloat16 [16, 2048, 1120], P('dp', 'seq'), may hold values from -6 to 6
- cotangent: bfloat16 [16, 2048, 1120], P('dp', 'seq'), may hold values from -6 to 6
- pad_mask: int32 [16, 2048], P('dp', 'seq'), may hold values from 0 to 1, as said below
- prefix_len: int32 [16], P('dp'), may hold values from 1 to 128
- norm_gains: float32 [2, 1120], replicated, may hold values from 0.5 to 1.5
- norm_shifts: float32 [2, 1120], replicated, may hold values from -1.8 to 1.8
- owner_map: int32 [192], replicated, may hold values from 0 to 191, as said below
- weight_copy: bfloat16 [192, 280, 280], P('dp'), may hold values from -1.8090681 to 1.8090681
- master: float32 [192, 280, 280], P('dp'), may hold values from -1.8090681 to 1.8090681
- average_weights: float32 [192, 280, 280], P('dp'), may hold values from -1.8090681 to 1.8090681
- stat_left: float32 [192, 280, 280], P('dp'), may hold values from -16.290909 to 36.654545, as said below
- stat_right: float32 [192, 280, 280], P('dp'), may hold values from -16.290909 to 36.654545, as said below
- root_left: float32 [192, 280, 280], P('dp'), may hold values from -3 to 5, as said below
- root_right: float32 [192, 280, 280], P('dp'), may hold values from -3 to 5, as said below
Outputs:
- block_out: bfloat16 [16, 2048, 1120], P('dp', 'seq')
- grad_input: float32 [16, 2048, 1120], P('dp', 'seq')
- norm_grad: float32 [4, 1120], replicated
- new_norms: float32 [4, 1120], replicated
- slot_grad: float32 [192, 280, 280], P('dp')
- new_left: float32 [192, 280, 280], P('dp')
- new_right: float32 [192, 280, 280], P('dp')
- new_master: float32 [192, 280, 280], P('dp')
- new_copy: bfloat16 [192, 280, 280], P('dp')
- new_average: float32 [192, 280, 280], P('dp')
Inputs may be any that keep to these rules, and one draw needn't show every extreme that they name: `pad_mask`: in each cell the ones come first, 512 or more of them; some cell has no zeros. `owner_map`: each block number appears once. `stat_left`: Symmetric. `stat_right`: Symmetric. `root_left`: Symmetric. `root_right`: Symmetric.
All inputs are finite; a program needn't handle non-finite values.
Results may differ from a plain program's by a relative error of at most 0.0085.
Values may be sent and summed in bfloat16 or wider, within the bound.
A program may use at most 448 MiB of HBM per device.

v0:
```python
import math
import jax
import jax.numpy as jnp
from jax import lax
from jax.sharding import PartitionSpec as P

HEADS = 20
GB = 256
PREFIX = 128
highest = lax.Precision.HIGHEST


def spread(block, axis, holder):
    block = jnp.where(lax.axis_index(axis) == holder, block, jnp.zeros_like(block))
    return lax.psum(block, axis)


def layer_norm(values, gain_row, shift_row):
    average = jnp.mean(values, axis=-1, keepdims=True)
    centred = values - average
    variance = jnp.mean(centred * centred, axis=-1, keepdims=True)
    return centred * lax.rsqrt(variance + 1e-05) * gain_row + shift_row


def gelu_tanh(values):
    return jax.nn.gelu(values, approximate=True)


def assemble(pieces, row_blocks, col_blocks):
    block_size = pieces.shape[-1]
    return (
        pieces.reshape(row_blocks, col_blocks, block_size, block_size)
        .transpose(0, 2, 1, 3)
        .reshape(row_blocks * block_size, col_blocks * block_size)
    )


def split_blocks(matrix, block_size):
    row_count, col_count = matrix.shape
    return (
        matrix.reshape(row_count // block_size, block_size, col_count // block_size, block_size)
        .transpose(0, 2, 1, 3)
        .reshape(-1, block_size, block_size)
    )


def matmul(left, right):
    return jnp.dot(left, right, preferred_element_type=jnp.float32)


def local(
    tokens,
    cotangent,
    pad_mask,
    prefix_len,
    norm_gains,
    norm_shifts,
    owner_map,
    weight_copy,
    master,
    average_weights,
    stat_left,
    stat_right,
    root_left,
    root_right,
):
    cell_count, group_len, features = tokens.shape
    row_count = cell_count * group_len
    head_size = features // HEADS
    per_group = group_len // GB
    score_scale = head_size ** (-0.5)
    slots = lax.all_gather(weight_copy, "dp", axis=0, tiled=True)
    block_count = slots.shape[0]
    block_size = slots.shape[-1]
    row_blocks = features // block_size
    col_blocks = (block_count - 4 * row_blocks * row_blocks) // (2 * row_blocks)
    square = row_blocks * row_blocks
    inverse = (
        jnp.zeros((block_count,), jnp.int32)
        .at[owner_map]
        .set(jnp.arange(block_count, dtype=jnp.int32))
    )
    blocks = jnp.take(slots, inverse, axis=0)
    w_query = assemble(blocks[0:square], row_blocks, row_blocks)
    w_key = assemble(blocks[square : 2 * square], row_blocks, row_blocks)
    w_value = assemble(blocks[2 * square : 3 * square], row_blocks, row_blocks)
    w_out = assemble(blocks[3 * square : 4 * square], row_blocks, row_blocks)
    w_up = assemble(
        blocks[4 * square : 4 * square + row_blocks * col_blocks], row_blocks, col_blocks
    )
    w_down = assemble(blocks[4 * square + row_blocks * col_blocks :], col_blocks, row_blocks)
    inputs = tokens.astype(jnp.float32).reshape(row_count, features)
    normed_one, norm_one_back = jax.vjp(layer_norm, inputs, norm_gains[0], norm_shifts[0])
    normed_in = normed_one.astype(jnp.bfloat16)
    queries = matmul(normed_in, w_query).astype(jnp.bfloat16)
    key_rows = matmul(normed_in, w_key).astype(jnp.bfloat16)
    value_rows = matmul(normed_in, w_value).astype(jnp.bfloat16)
    block_shape = (cell_count, per_group, GB, HEADS, head_size)
    query_blocks = queries.reshape(block_shape)
    key_blocks = key_rows.reshape(block_shape)
    value_blocks = value_rows.reshape(block_shape)
    key_cells = key_rows.reshape(cell_count, group_len, HEADS, head_size)
    value_cells = value_rows.reshape(cell_count, group_len, HEADS, head_size)
    prefix_keys, prefix_values = (
        spread(key_cells[:, :PREFIX], "seq", 0),
        spread(value_cells[:, :PREFIX], "seq", 0),
    )
    seq_index = lax.axis_index("seq")
    position = seq_index * group_len + jnp.arange(group_len, dtype=jnp.int32)
    alive_keys = jnp.where(
        position[None, :] < PREFIX, position[None, :] < prefix_len[:, None], pad_mask == 1
    )
    prefix_alive = jnp.arange(PREFIX, dtype=jnp.int32)[None, :] < prefix_len[:, None]
    offsets = jnp.arange(GB)
    local_seen = alive_keys.reshape(cell_count, per_group, 1, 1, GB) & (
        offsets[:, None] >= offsets[None, :]
    )
    later_block = seq_index * per_group + jnp.arange(per_group) > 0
    prefix_seen = prefix_alive[:, None, None, None, :] & later_block[None, :, None, None, None]
    visible = jnp.concatenate(
        [jnp.broadcast_to(prefix_seen, (cell_count, per_group, 1, GB, PREFIX)), local_seen], axis=-1
    )

    def score_rows():
        raw_prefix = jnp.einsum(
            "cnqhd,ckhd->cnhqk", query_blocks, prefix_keys, preferred_element_type=jnp.float32
        )
        raw_local = jnp.einsum(
            "cnqhd,cnkhd->cnhqk", query_blocks, key_blocks, preferred_element_type=jnp.float32
        )
        return jnp.where(
            visible, jnp.concatenate([raw_prefix, raw_local], axis=-1) * score_scale, -1e30
        )

    scores = score_rows()
    row_max = jnp.max(scores, axis=-1, keepdims=True)
    log_total = row_max + jnp.log(jnp.sum(jnp.exp(scores - row_max), axis=-1, keepdims=True))
    weights_low = jnp.exp(scores - log_total).astype(jnp.bfloat16)
    attended = jnp.einsum(
        "cnhqk,ckhd->cnqhd",
        weights_low[..., :PREFIX],
        prefix_values,
        preferred_element_type=jnp.float32,
    )
    attended = attended + jnp.einsum(
        "cnhqk,cnkhd->cnqhd",
        weights_low[..., PREFIX:],
        value_blocks,
        preferred_element_type=jnp.float32,
    )
    attended_low = attended.reshape(row_count, features).astype(jnp.bfloat16)
    middle = inputs + matmul(attended_low, w_out)
    normed_two, norm_two_back = jax.vjp(layer_norm, middle, norm_gains[1], norm_shifts[1])
    normed_mid = normed_two.astype(jnp.bfloat16)
    up_pre = matmul(normed_mid, w_up)
    activated, gelu_back = jax.vjp(gelu_tanh, up_pre)
    activated_low = activated.astype(jnp.bfloat16)
    block_out = (
        (middle + matmul(activated_low, w_down))
        .astype(jnp.bfloat16)
        .reshape(cell_count, group_len, features)
    )
    grad_rows = cotangent.astype(jnp.float32).reshape(row_count, features)
    grad_low = cotangent.reshape(row_count, features)
    grad_down = matmul(activated_low.T, grad_low)
    grad_act = matmul(grad_low, w_down.T)
    grad_pre = gelu_back(grad_act)[0].astype(jnp.bfloat16)
    grad_up = matmul(normed_mid.T, grad_pre)
    grad_mid_in = matmul(grad_pre, w_up.T)
    grad_middle_n, grad_gain_two, grad_shift_two = norm_two_back(grad_mid_in)
    grad_middle = grad_rows + grad_middle_n
    grad_branch = grad_middle.astype(jnp.bfloat16)
    grad_out = matmul(attended_low.T, grad_branch)
    grad_att = matmul(grad_branch, w_out.T).astype(jnp.bfloat16).reshape(block_shape)
    key_weights = jnp.exp(score_rows() - log_total)
    weights_again = key_weights.astype(jnp.bfloat16)
    grad_prob = jnp.concatenate(
        [
            jnp.einsum(
                "cnqhd,ckhd->cnhqk", grad_att, prefix_values, preferred_element_type=jnp.float32
            ),
            jnp.einsum(
                "cnqhd,cnkhd->cnhqk", grad_att, value_blocks, preferred_element_type=jnp.float32
            ),
        ],
        axis=-1,
    )
    grad_score = key_weights * (
        grad_prob - jnp.sum(key_weights * grad_prob, axis=-1, keepdims=True)
    )
    grad_raw = (grad_score * score_scale).astype(jnp.bfloat16)
    grad_raw_prefix = grad_raw[..., :PREFIX]
    grad_raw_local = grad_raw[..., PREFIX:]
    grad_query = jnp.einsum(
        "cnhqk,ckhd->cnqhd", grad_raw_prefix, prefix_keys, preferred_element_type=jnp.float32
    )
    grad_query = grad_query + jnp.einsum(
        "cnhqk,cnkhd->cnqhd", grad_raw_local, key_blocks, preferred_element_type=jnp.float32
    )
    grad_key = jnp.einsum(
        "cnhqk,cnqhd->cnkhd", grad_raw_local, query_blocks, preferred_element_type=jnp.float32
    )
    grad_value = jnp.einsum(
        "cnhqk,cnqhd->cnkhd",
        weights_again[..., PREFIX:],
        grad_att,
        preferred_element_type=jnp.float32,
    )
    grad_key_pre = jnp.einsum(
        "cnhqk,cnqhd->ckhd", grad_raw_prefix, query_blocks, preferred_element_type=jnp.float32
    )
    grad_value_pre = jnp.einsum(
        "cnhqk,cnqhd->ckhd",
        weights_again[..., :PREFIX],
        grad_att,
        preferred_element_type=jnp.float32,
    )
    summed_key, summed_value = lax.psum((grad_key_pre, grad_value_pre), "seq")
    is_owner = (seq_index == 0).astype(jnp.float32)
    grad_key = (
        grad_key.reshape(cell_count, group_len, features)
        .at[:, :PREFIX]
        .add(is_owner * summed_key.reshape(cell_count, PREFIX, features))
    )
    grad_value = (
        grad_value.reshape(cell_count, group_len, features)
        .at[:, :PREFIX]
        .add(is_owner * summed_value.reshape(cell_count, PREFIX, features))
    )
    query_grad_low = grad_query.reshape(row_count, features).astype(jnp.bfloat16)
    key_grad_low = grad_key.reshape(row_count, features).astype(jnp.bfloat16)
    value_grad_low = grad_value.reshape(row_count, features).astype(jnp.bfloat16)
    grad_wq = matmul(normed_in.T, query_grad_low)
    grad_wk = matmul(normed_in.T, key_grad_low)
    grad_wv = matmul(normed_in.T, value_grad_low)
    grad_normed = (
        matmul(query_grad_low, w_query.T)
        + matmul(key_grad_low, w_key.T)
        + matmul(value_grad_low, w_value.T)
    )
    grad_in_n, grad_gain_one, grad_shift_one = norm_one_back(grad_normed)
    grad_input = (grad_middle + grad_in_n).reshape(cell_count, group_len, features)
    grad_scale = 1.0 / math.sqrt(row_count * lax.axis_size("dp") * lax.axis_size("seq"))
    norm_terms = (
        jnp.stack([grad_gain_one, grad_shift_one, grad_gain_two, grad_shift_two]) * grad_scale
    )
    norm_grad = lax.psum(norm_terms, ("dp", "seq"))
    params = jnp.stack([norm_gains[0], norm_shifts[0], norm_gains[1], norm_shifts[1]])
    new_norms = params - 0.1 * norm_grad * lax.rsqrt(jnp.mean(norm_grad * norm_grad) + 1e-06)
    grad_blocks = (
        jnp.concatenate(
            [
                split_blocks(matrix, block_size)
                for matrix in (grad_wq, grad_wk, grad_wv, grad_out, grad_up, grad_down)
            ],
            axis=0,
        )
        * grad_scale
    )
    ordered = jnp.take(grad_blocks, owner_map, axis=0)
    owned_part = lax.psum_scatter(ordered, "dp", scatter_dimension=0, tiled=True)
    slot_grad = lax.psum(owned_part, "seq")
    new_left = (
        0.5 * stat_left
        + 0.5 * jnp.einsum("sij,skj->sik", slot_grad, slot_grad, precision=highest) / block_size
    )
    new_right = (
        0.5 * stat_right
        + 0.5 * jnp.einsum("sji,sjk->sik", slot_grad, slot_grad, precision=highest) / block_size
    )
    right_part = jnp.einsum("sij,sjk->sik", slot_grad, root_right, precision=highest)
    precond = jnp.einsum("sij,sjk->sik", root_left, right_part, precision=highest)
    new_master = master - 0.03 * precond
    new_copy = new_master.astype(jnp.bfloat16)
    new_average = 0.8 * average_weights + 0.2 * new_master
    return (
        block_out,
        grad_input,
        norm_grad,
        new_norms,
        slot_grad,
        new_left,
        new_right,
        new_master,
        new_copy,
        new_average,
    )


def solution(mesh):
    in_specs = (
        P("dp", "seq", None),
        P("dp", "seq", None),
        P("dp", "seq"),
        P("dp"),
        P(),
        P(),
        P(),
        P("dp", None, None),
        P("dp", None, None),
        P("dp", None, None),
        P("dp", None, None),
        P("dp", None, None),
        P("dp", None, None),
        P("dp", None, None),
    )
    out_specs = (
        P("dp", "seq", None),
        P("dp", "seq", None),
        P(),
        P(),
        P("dp", None, None),
        P("dp", None, None),
        P("dp", None, None),
        P("dp", None, None),
        P("dp", None, None),
        P("dp", None, None),
    )
    return jax.shard_map(local, mesh=mesh, in_specs=in_specs, out_specs=out_specs, check_vma=False)
```

profile of v0, /device:TPU:0, one launch (start us, length us, event | category | flops | bytes accessed | tf_op | source)
XLA Modules:
  0.0 2638.7 jit_solution(1818044440257464110)
XLA Ops:
  16.7 420.8 %all-gather.2.cloned.1.call-done = bf16[192,280,280]{2,1,0:T(8,128)(2,1)} async-done(((bf16[12,280,280]{2,1,0:T(8,128)(2,1)}), bf16[192,280,280]{2,1,0:T(8,128)(2,1)}) %all-gather.2.cloned.1.call-update) | async-done | bytes 30105616 | tf_op jit(solution)/shard_map/all_gather | solution.py:72
  437.5 28.3 %gather_fusion = bf16[192,280,280]{2,1,0:T(8,128)(2,1)} fusion(bf16[192,280,280]{2,1,0:T(8,128)(2,1)} %all-gather.2.cloned.1.call-done, s32[1024]{0:T(1024)S(1)} %pad_clamp_fusion.1), kind=kCustom, calls=%fused_computation | custom fusion | bytes 60211968 | tf_op jit(solution)/shard_map/jit(_take)/gather | solution.py:83
  465.8 28.1 %broadcast_select_fusion.1 = bf16[192,280,280]{2,1,0:T(8,128)(2,1)} fusion(bf16[192,280,280]{2,1,0:T(8,128)(2,1)} %gather_fusion, pred[192]{0:T(512)(128)(4,1)S(1)} %compare_and_fusion.1), kind=kLoop, calls=%fused_computation.5 | loop fusion | flops 15052800 | bytes 60211392 | tf_op jit(solution)/shard_map/jit(_take)/select_n | solution.py:83
  493.9 9.3 fusion.111
  503.2 21.0 fusion.110
  527.4 6.3 reshape.760
  538.7 6.3 reshape.764
  545.0 6.7 convolution_convert_fusion.3
  551.7 5.1 convolution_convert_fusion.2
  559.9 6.3 reshape.768
  569.7 6.6 convolution_convert_fusion.1
  576.3 5.6 reshape.772
  589.3 5.9 copy.248
  595.2 6.3 reshape.775
  601.5 22.4 copy.115
  623.9 21.1 reshape.779
  644.9 14.3 copy.247
  659.3 21.4 reshape.777
  680.7 11.6 convolution_bitcast_fusion.1
  695.0 13.9 fusion.108
  709.7 6.5 exponential_reduce_fusion
  716.3 9.9 fusion.1
  726.2 5.2 fusion.22
  741.5 26.2 fusion.16
  767.8 31.0 %fusion.8 = bf16[1024,4480]{1,0:T(8,128)(2,1)} fusion(f32[1024,4480]{1,0:T(8,128)} %get-tuple-element.100, bf16[4480,1120]{0,1:T(8,128)(2,1)} %reshape.779, bf16[1,1024,1120]{1,2,0:T(8,128)(2,1)S(1)} %copy-done.12), kind=kOutput, calls=%fused_computation.23 | convolution fusion | flops 10367795200 | bytes 39854080 | tf_op jit(solution)/shard_map/dot_general | solution.py:48
  798.8 19.8 multiply_reduce_fusion.1
  832.3 9.6 convolution_bitcast_fusion.4
  842.0 8.6 convolution_bitcast_fusion
  850.6 5.4 convolution_bitcast_fusion.2
  856.0 5.2 fusion.74
  861.1 20.7 multiply_reduce_fusion
  881.8 22.1 multiply_convert_fusion
  903.9 5.5 copy-done.1
  912.1 8.7 fusion.20
  920.8 9.6 convolution_bitcast_fusion.5
  930.5 18.1 fusion.103
  948.6 5.1 copy.134
  953.7 6.5 reshape.790
  977.7 6.5 reshape.787
  988.5 28.5 %reshape.801 = f32[4,280,16,280]{3,2,1,0:T(8,128)} reshape(f32[1120,4480]{1,0:T(8,128)} %fusion.103) | data formatting | bytes 40140800 | tf_op jit(solution)/shard_map/reshape | solution.py:41
  1017.1 27.0 %copy.138 = f32[4,280,16,280]{3,1,2,0:T(8,128)} copy(f32[4,280,16,280]{3,2,1,0:T(8,128)} %reshape.801) | data formatting | bytes 40140800 | tf_op jit(solution)/shard_map/reshape | solution.py:41
  1044.0 12.7 copy.139
  1056.8 20.0 fusion.117
  1081.6 5.8 fusion.116
  1091.6 5.7 fusion.120
  1121.3 7.6 fusion.115
  1132.6 6.8 constant_dynamic-update-slice_fusion.3
  1139.4 6.4 constant_dynamic-update-slice_fusion.2
  1145.9 9.4 constant_dynamic-update-slice_fusion.1
  1155.3 20.5 constant_dynamic-update-slice_fusion
  1175.8 55.9 %broadcast_multiply_fusion = f32[192,280,280]{2,1,0:T(8,128)} fusion(f32[192,280,280]{2,1,0:T(8,128)} %constant_dynamic-update-slice_fusion), kind=kLoop, calls=%fused_computation.4 | loop fusion | flops 15052800 | bytes 120422400 | tf_op jit(solution)/shard_map/mul | solution.py:251
  1231.7 56.4 %gather_fusion.1 = f32[192,280,280]{2,1,0:T(8,128)} fusion(f32[192,280,280]{2,1,0:T(8,128)} %broadcast_multiply_fusion, s32[1024]{0:T(1024)} %pad_clamp_fusion), kind=kCustom, calls=%fused_computation.1 | custom fusion | bytes 120423168 | tf_op jit(solution)/shard_map/jit(_take)/gather | solution.py:260
  1288.1 54.1 %broadcast_select_fusion = f32[192,280,280]{2,1,0:T(8,128)} fusion(f32[192,280,280]{2,1,0:T(8,128)} %gather_fusion.1, pred[192]{0:T(512)(128)(4,1)S(1)} %copy-done.57), kind=kLoop, calls=%fused_computation.3 | loop fusion | flops 15052800 | bytes 120422592 | tf_op jit(solution)/shard_map/jit(_take)/select_n | solution.py:260
  1342.2 1134.6 %reduce-scatter.2.cloned.1.call-done = f32[12,280,280]{2,1,0:T(8,128)} async-done(((f32[192,280,280]{2,1,0:T(8,128)}), f32[12,280,280]{2,1,0:T(8,128)}) %reduce-scatter.2.cloned.1.call-update) | async-done | bytes 3763216 | tf_op jit(solution)/shard_map/reduce_scatter | solution.py:261
  2476.8 6.1 copy.143
  2483.0 6.5 copy.142
  2489.6 19.8 fusion.54
  2509.4 39.9 %psum.46 = f32[4,1120]{1,0:T(4,128)S(1)} all-reduce(f32[4,1120]{1,0:T(4,128)S(1)} %maximum_multiply_fusion.1), channel_id=1, replica_groups=mesh['dp'=16,'seq'=2] {'dp','seq'}, use_global_device_ids=true, to_apply=%region_20.21 | all-reduce | flops 4480 | bytes 35840 | tf_op jit(solution)/shard_map/psum | solution.py:247
  2551.3 14.1 fusion.118
  2565.4 17.3 multiply_add_fusion
  2582.7 6.1 copy.144
  2591.6 6.2 copy.146
  2597.8 16.9 multiply_add_fusion.2
  2614.7 14.9 multiply_add_fusion.1
  (258 shorter events, 125.6 us)
Async XLA Ops:
  7.2 6.6 copy-start.5
  7.2 8.3 copy-start.51
  7.2 8.2 copy-start.52
  7.2 430.3 %all-gather.2.cloned.1.call-start = ((), (), s32[]{:S(2)}) async-start(), calls=%async_computation.1 | async-start | bytes 43868160 | tf_op jit(solution)/shard_map/all_gather | solution.py:72
  7.9 684.3 %all-reduce.10.cloned.1.call-start = ((), (), s32[]{:S(2)}) async-start(), calls=%async_computation.5 | async-start | bytes 1146880 | tf_op jit(solution)/shard_map/psum | solution.py:15
  14.2 555.5 %copy-start.34 = (f32[1024]{0:T(1024)}, f32[1024]{0:T(1024)S(1)}, u32[]{:S(2)}) copy-start(f32[1024]{0:T(1024)S(1)} %broadcast_multiply_fusion.4) | copy-start | bytes 12292
  15.5 554.3 %copy-start.40 = (f32[1024]{0:T(1024)}, f32[1024]{0:T(1024)S(1)}, u32[]{:S(2)}) copy-start(f32[1024]{0:T(1024)S(1)} %fusion.95) | copy-start | bytes 12292
  16.7 553.0 %copy-start.32 = (f32[1120]{0:T(1024)}, f32[1120]{0:T(1024)S(1)}, u32[]{:S(2)}) copy-start(f32[1120]{0:T(1024)S(1)} %get-tuple-element.104) | copy-start | bytes 13444
  16.7 553.0 %copy-start.42 = (f32[1120]{0:T(1024)}, f32[1120]{0:T(1024)S(1)}, u32[]{:S(2)}) copy-start(f32[1120]{0:T(1024)S(1)} %get-tuple-element.73) | copy-start | bytes 13444
  545.0 6.7 copy-start.16
  569.7 517.7 %all-reduce.8.cloned.1.call-start = ((), (), s32[]{:S(2)}) async-start(), calls=%async_computation.4 | async-start | bytes 2293760 | tf_op jit(solution)/shard_map/psum | solution.py:218
  589.3 103.0 %copy-start.2 = (bf16[4,256,20,56]{1,0,3,2:T(4,128)(2,1)}, bf16[4,256,20,56]{1,0,3,2:T(4,128)(2,1)S(1)}, u32[]{:S(2)}) copy-start(bf16[4,256,20,56]{1,0,3,2:T(4,128)(2,1)S(1)} %reshape.769) | copy-start | bytes 6881284
  692.3 16.6 slice-start
  692.3 16.6 slice-start.1
  695.0 21.3 copy-start
  695.0 14.0 slice-start.2
  695.0 14.0 slice-start.3
  695.0 14.7 slice-start.4
  716.3 9.9 copy-start.10
  740.9 77.7 %copy-start.8 = (f32[1024,1120]{0,1:T(8,128)}, f32[1024,1120]{0,1:T(8,128)S(1)}, u32[]{:S(2)}) copy-start(f32[1024,1120]{0,1:T(8,128)S(1)} %get-tuple-element.95) | copy-start | bytes 13762564
  741.5 26.3 copy-start.12
  832.3 9.6 copy-start.11
  881.8 27.6 %copy-start.3 = (bf16[4,256,20,56]{1,0,3,2:T(4,128)(2,1)S(1)}, bf16[4,256,20,56]{1,0,3,2:T(4,128)(2,1)}, u32[]{:S(2)}) copy-start(bf16[4,256,20,56]{1,0,3,2:T(4,128)(2,1)} %copy-done.2) | copy-start | bytes 6881284
  912.1 18.3 slice-start.16
  920.8 9.6 slice-start.17
  920.8 9.6 copy-start.54
  920.8 27.8 %slice-start.18 = ((s8[4587520]{0:T(1024)(128)(4,1)}), s8[4194304]{0:T(1024)(128)(4,1)S(1)}, s32[]{:S(2)}) async-start(s8[4587520]{0:T(1024)(128)(4,1)} %bitcast.354), calls=%async_computation.24 | async-start | bytes 8388608
  930.4 18.1 slice-start.19
  960.2 12.5 slice-start.20
  964.7 8.0 slice-start.21
  1044.0 12.7 copy-start.13
  1056.7 1420.1 %reduce-scatter.2.cloned.1.call-start = ((), (), s32[]{:S(2)}) async-start(), calls=%async_computation.2 | async-start | bytes 87736320 | tf_op jit(solution)/shard_map/reduce_scatter | solution.py:261
  1056.8 20.0 copy-start.17
  1056.8 20.0 copy-start.22
  1089.6 9.2 slice-start.22
  1091.6 5.8 copy-start.24
  1091.6 7.2 copy-start.7
  1091.6 7.2 copy-start.15
  1091.6 7.2 copy-start.33
  1091.6 7.2 copy-start.35
  1091.6 7.2 slice-start.23
  1097.4 8.6 slice-start.14
  1098.9 7.1 slice-start.15
  1110.3 7.1 copy-start.28
  1121.3 24.5 slice-start.7
  1121.3 24.5 slice-start.8
  1121.3 24.5 slice-start.9
  1128.9 16.9 slice-start.10
  1132.6 13.2 slice-start.11
  1132.6 13.2 slice-start.12
  1139.4 6.4 slice-start.13
  1231.7 56.4 %copy-start.57 = (pred[192]{0:T(512)(128)(4,1)S(1)}, pred[192]{0:T(512)(128)(4,1)}, u32[]{:S(2)}) copy-start(pred[192]{0:T(512)(128)(4,1)} %compare_and_fusion) | copy-start | bytes 580
  1342.2 1209.1 %all-reduce.6.cloned.1.call-start = ((), (), s32[]{:S(2)}) async-start(), calls=%async_computation.3 | async-start | bytes 10321920 | tf_op jit(solution)/shard_map/psum | solution.py:262
  2483.0 6.5 copy-start.56
  2483.0 6.5 copy-start.55
  2489.5 19.9 copy-start.46
  2489.5 19.9 copy-start.45
  2489.5 61.1 %copy-start.47 = (f32[1,1120]{1,0:T(1,128)S(1)}, f32[1,1120]{1,0:T(1,128)}, u32[]{:S(2)}) copy-start(f32[1,1120]{1,0:T(1,128)} %get-tuple-element.91) | copy-start | bytes 13444
  2489.5 61.1 %copy-start.48 = (f32[1,1120]{1,0:T(1,128)S(1)}, f32[1,1120]{1,0:T(1,128)}, u32[]{:S(2)}) copy-start(f32[1,1120]{1,0:T(1,128)} %get-tuple-element.93) | copy-start | bytes 13444
  2489.5 61.1 %copy-start.49 = (f32[1,1120]{1,0:T(1,128)S(1)}, f32[1,1120]{1,0:T(1,128)}, u32[]{:S(2)}) copy-start(f32[1,1120]{1,0:T(1,128)} %get-tuple-element.102) | copy-start | bytes 13444
  2489.6 61.1 %copy-start.50 = (f32[1,1120]{1,0:T(1,128)S(1)}, f32[1,1120]{1,0:T(1,128)}, u32[]{:S(2)}) copy-start(f32[1,1120]{1,0:T(1,128)} %get-tuple-element.103) | copy-start | bytes 13444
  2549.3 16.1 copy-start.31
  2591.6 23.1 slice-start.5
  2597.8 16.9 slice-start.6
  (23 other events, 84.3 us)
Sparse Core Ops, SparseCore 0:
  10.8 426.5 all-gather.1
  569.8 17.0 all-reduce.9
  1056.8 18.0 all-reduce.7
  1342.3 1134.4 reduce-scatter.1
  2479.3 29.0 all-reduce.5
where the time goes:
time: 2650 us; the launch traced here: 2640 us
  waiting for transfers between devices  1560 us (59%)
  local copies, waits for them, and re-layouts  452 us (17%)
  matrix products  338 us (13%)
  other arithmetic  236 us (9%)
  blocking collectives  39.9 us (2%)
    reduce_scatter x1, waiting for transfers between devices, local(): lax.psum_scatter(ordered, 'dp', scatter_dimension=0, tiled=True)  1130 us
    all_gather x1, waiting for transfers between devices, local(): slots = lax.all_gather(weight_copy, 'dp', axis=0, tiled=True)  421 us
    dot_general x18, matrix products, matmul(): return jnp.dot(left, right, preferred_element_type=jnp.float32)  197 us
    unnamed x179, local copies, waits for them, and re-layouts  81.6 us
    reshape x6, local copies, waits for them, and re-layouts, assemble(): return pieces.reshape(row_blocks, col_blocks, block_size, block_size).tra...  67.7 us
    gather x1, local copies, waits for them, and re-layouts, local(): ordered = jnp.take(grad_blocks, owner_map, axis=0)  56.4 us
    mul x1, other arithmetic, local(): jnp.concatenate([split_blocks(matrix, block_size) for matrix in (grad_wq,...  55.9 us
    reshape x2, local copies, waits for them, and re-layouts, split_blocks(): matrix.reshape(row_count // block_size, block_size, col_count // block_si...  55.5 us
  transfers between devices with their start and end apart: 5, of which 2 were waited for; matrix products, arithmetic and copies ran while one was open for 7% of the time, Pallas kernels for 0%

commit v1 on v0

--- a/solution.py
+++ b/solution.py
@@ -8,6 +8,17 @@
 GB = 256
 PREFIX = 128
 highest = lax.Precision.HIGHEST
+
+
+def collect(x, axis, dim):
+    ways = lax.axis_size(axis)
+    pieces = [x]
+    for far in range(1, ways):
+        pieces.append(
+            lax.ppermute(pieces[far - 1], axis, [(d, (d - 1) % ways) for d in range(ways)])
+        )
+    line = jnp.concatenate(pieces, axis=dim)
+    return jnp.roll(line, lax.axis_index(axis) * x.shape[dim], axis=dim)
 
 
 def spread(block, axis, holder):
@@ -69,7 +80,7 @@
     head_size = features // HEADS
     per_group = group_len // GB
     score_scale = head_size ** (-0.5)
-    slots = lax.all_gather(weight_copy, "dp", axis=0, tiled=True)
+    slots = collect(weight_copy, "dp", 0)
     block_count = slots.shape[0]
     block_size = slots.shape[-1]
     row_blocks = features // block_size

time: 2650 us -> 3150 us (1.19)
  waiting for transfers between devices: 1560 us -> 1850 us
  local copies, waits for them, and re-layouts: 452 us -> 563 us
  starting transfers between devices: 0.2 us -> 92.6 us
    ppermute x0 -> x15, waiting for transfers between devices: none -> 714 us  [collect(): lax.ppermute(pieces[far - 1], axis, [(d, (d - 1) % ways) for d in range(w...]
    all_gather x1 -> x0, waiting for transfers between devices: 421 us -> none  [local(): slots = lax.all_gather(weight_copy, 'dp', axis=0, tiled=True)]
    ppermute x0 -> x15, starting transfers between devices: none -> 92.4 us  [collect(): lax.ppermute(pieces[far - 1], axis, [(d, (d - 1) % ways) for d in range(w...]
    unnamed x179 -> x254, local copies, waits for them, and re-layouts: 81.6 us -> 163 us
  transfers between devices with their start and end apart: 5 -> 19, of which waited for: 2 -> 16; matrix products, arithmetic and copies ran while one was open for 7% -> 7% of each run, Pallas kernels for 0% -> 0%
where the time goes in v1:
time: 3150 us; the launch traced here: 3140 us
  waiting for transfers between devices  1850 us (59%)
  local copies, waits for them, and re-layouts  563 us (18%)
  matrix products  338 us (11%)
  other arithmetic  237 us (8%)
  starting transfers between devices  92.6 us (3%)
  blocking collectives  39.9 us (1%)
    reduce_scatter x1, waiting for transfers between devices, local(): lax.psum_scatter(ordered, 'dp', scatter_dimension=0, tiled=True)  1140 us
    ppermute x15, waiting for transfers between devices, collect(): lax.ppermute(pieces[far - 1], axis, [(d, (d - 1) % ways) for d in range(w...  714 us
    dot_general x18, matrix products, matmul(): return jnp.dot(left, right, preferred_element_type=jnp.float32)  196 us
    unnamed x254, local copies, waits for them, and re-layouts  163 us
    ppermute x15, starting transfers between devices, collect(): lax.ppermute(pieces[far - 1], axis, [(d, (d - 1) % ways) for d in range(w...  92.4 us
    reshape x6, local copies, waits for them, and re-layouts, assemble(): return pieces.reshape(row_blocks, col_blocks, block_size, block_size).tra...  67.7 us
  transfers between devices with their start and end apart: 19, of which 16 were waited for; matrix products, arithmetic and copies ran while one was open for 7% of the time, Pallas kernels for 0%

profile of v1, /device:TPU:0, one launch (start us, length us, event | category | flops | bytes accessed | tf_op | source)
XLA Modules:
  0.0 3138.7 jit_solution(18233350251541979582)
XLA Ops:
  7.2 7.0 collective-permute-start
  14.2 55.6 %collective-permute-done = bf16[12,280,280]{2,1,0:T(8,128)(2,1)S(1)} collective-permute-done((bf16[12,280,280]{2,1,0:T(8,128)(2,1)}, bf16[12,280,280]{2,1,0:T(8,128)(2,1)S(1)}, u32[]{:S(2)}, u32[]{:S(2)}) %collective-permute-start) | collective-permute-done | bytes 1881632 | tf_op jit(solution)/shard_map/ppermute | solution.py:18
  77.2 54.4 %collective-permute-done.1 = bf16[12,280,280]{2,1,0:T(8,128)(2,1)S(1)} collective-permute-done((bf16[12,280,280]{2,1,0:T(8,128)(2,1)S(1)}, bf16[12,280,280]{2,1,0:T(8,128)(2,1)S(1)}, u32[]{:S(2)}, u32[]{:S(2)}) %collective-permute-start.1) | collective-permute-done | bytes 1881632 | tf_op jit(solution)/shard_map/ppermute | solution.py:18
  139.2 53.5 %collective-permute-done.2 = bf16[12,280,280]{2,1,0:T(8,128)(2,1)S(1)} collective-permute-done((bf16[12,280,280]{2,1,0:T(8,128)(2,1)S(1)}, bf16[12,280,280]{2,1,0:T(8,128)(2,1)S(1)}, u32[]{:S(2)}, u32[]{:S(2)}) %collective-permute-start.2) | collective-permute-done | bytes 1881632 | tf_op jit(solution)/shard_map/ppermute | solution.py:18
  200.2 52.5 %collective-permute-done.3 = bf16[12,280,280]{2,1,0:T(8,128)(2,1)S(1)} collective-permute-done((bf16[12,280,280]{2,1,0:T(8,128)(2,1)S(1)}, bf16[12,280,280]{2,1,0:T(8,128)(2,1)S(1)}, u32[]{:S(2)}, u32[]{:S(2)}) %collective-permute-start.3) | collective-permute-done | bytes 1881632 | tf_op jit(solution)/shard_map/ppermute | solution.py:18
  260.3 51.6 %collective-permute-done.4 = bf16[12,280,280]{2,1,0:T(8,128)(2,1)S(1)} collective-permute-done((bf16[12,280,280]{2,1,0:T(8,128)(2,1)S(1)}, bf16[12,280,280]{2,1,0:T(8,128)(2,1)S(1)}, u32[]{:S(2)}, u32[]{:S(2)}) %collective-permute-start.4) | collective-permute-done | bytes 1881632 | tf_op jit(solution)/shard_map/ppermute | solution.py:18
  319.4 50.7 %collective-permute-done.5 = bf16[12,280,280]{2,1,0:T(8,128)(2,1)S(1)} collective-permute-done((bf16[12,280,280]{2,1,0:T(8,128)(2,1)S(1)}, bf16[12,280,280]{2,1,0:T(8,128)(2,1)S(1)}, u32[]{:S(2)}, u32[]{:S(2)}) %collective-permute-start.5) | collective-permute-done | bytes 1881632 | tf_op jit(solution)/shard_map/ppermute | solution.py:18
  377.7 49.8 %collective-permute-done.6 = bf16[12,280,280]{2,1,0:T(8,128)(2,1)S(1)} collective-permute-done((bf16[12,280,280]{2,1,0:T(8,128)(2,1)S(1)}, bf16[12,280,280]{2,1,0:T(8,128)(2,1)S(1)}, u32[]{:S(2)}, u32[]{:S(2)}) %collective-permute-start.6) | collective-permute-done | bytes 1881632 | tf_op jit(solution)/shard_map/ppermute | solution.py:18
  435.0 48.8 %collective-permute-done.7 = bf16[12,280,280]{2,1,0:T(8,128)(2,1)S(1)} collective-permute-done((bf16[12,280,280]{2,1,0:T(8,128)(2,1)S(1)}, bf16[12,280,280]{2,1,0:T(8,128)(2,1)S(1)}, u32[]{:S(2)}, u32[]{:S(2)}) %collective-permute-start.7) | collective-permute-done | bytes 1881632 | tf_op jit(solution)/shard_map/ppermute | solution.py:18
  491.5 48.6 %collective-permute-done.8 = bf16[12,280,280]{2,1,0:T(8,128)(2,1)S(1)} collective-permute-done((bf16[12,280,280]{2,1,0:T(8,128)(2,1)S(1)}, bf16[12,280,280]{2,1,0:T(8,128)(2,1)S(1)}, u32[]{:S(2)}, u32[]{:S(2)}) %collective-permute-start.8) | collective-permute-done | bytes 1881632 | tf_op jit(solution)/shard_map/ppermute | solution.py:18
  547.6 48.6 %collective-permute-done.9 = bf16[12,280,280]{2,1,0:T(8,128)(2,1)S(1)} collective-permute-done((bf16[12,280,280]{2,1,0:T(8,128)(2,1)S(1)}, bf16[12,280,280]{2,1,0:T(8,128)(2,1)S(1)}, u32[]{:S(2)}, u32[]{:S(2)}) %collective-permute-start.9) | collective-permute-done | bytes 1881632 | tf_op jit(solution)/shard_map/ppermute | solution.py:18
  603.8 49.8 %collective-permute-done.10 = bf16[12,280,280]{2,1,0:T(8,128)(2,1)} collective-permute-done((bf16[12,280,280]{2,1,0:T(8,128)(2,1)S(1)}, bf16[12,280,280]{2,1,0:T(8,128)(2,1)}, u32[]{:S(2)}, u32[]{:S(2)}) %collective-permute-start.10) | collective-permute-done | bytes 1881632 | tf_op jit(solution)/shard_map/ppermute | solution.py:18
  660.4 49.4 %collective-permute-done.11 = bf16[12,280,280]{2,1,0:T(8,128)(2,1)} collective-permute-done((bf16[12,280,280]{2,1,0:T(8,128)(2,1)}, bf16[12,280,280]{2,1,0:T(8,128)(2,1)}, u32[]{:S(2)}, u32[]{:S(2)}) %collective-permute-start.11) | collective-permute-done | bytes 1881632 | tf_op jit(solution)/shard_map/ppermute | solution.py:18
  721.8 44.1 %collective-permute-done.12 = bf16[12,280,280]{2,1,0:T(8,128)(2,1)} collective-permute-done((bf16[12,280,280]{2,1,0:T(8,128)(2,1)}, bf16[12,280,280]{2,1,0:T(8,128)(2,1)}, u32[]{:S(2)}, u32[]{:S(2)}) %collective-permute-start.12) | collective-permute-done | bytes 1881632 | tf_op jit(solution)/shard_map/ppermute | solution.py:18
  783.6 38.3 %collective-permute-done.13 = bf16[12,280,280]{2,1,0:T(8,128)(2,1)S(1)} collective-permute-done((bf16[12,280,280]{2,1,0:T(8,128)(2,1)}, bf16[12,280,280]{2,1,0:T(8,128)(2,1)S(1)}, u32[]{:S(2)}, u32[]{:S(2)}) %collective-permute-start.13) | collective-permute-done | bytes 1881632 | tf_op jit(solution)/shard_map/ppermute | solution.py:18
  822.0 6.4 collective-permute-start.14
  852.8 18.3 collective-permute-done.14
  906.0 28.2 constant_dynamic-slice_fusion
  934.3 28.1 gather_fusion
  962.4 28.2 broadcast_select_fusion.1
  990.5 9.3 fusion.111
  999.9 21.1 fusion.110
  1041.7 6.7 convolution_convert_fusion.3
  1066.4 6.6 convolution_convert_fusion.1
  1098.1 22.4 copy.70
  1120.5 21.1 reshape.779
  1141.6 14.3 copy.200
  1155.9 21.5 reshape.777
  1177.4 11.6 convolution_bitcast_fusion.1
  1191.8 13.9 fusion.108
  1206.5 6.5 exponential_reduce_fusion
  1213.1 9.9 fusion.1
  1238.3 26.3 fusion.16
  1264.6 30.9 fusion.8
  1295.5 19.8 multiply_reduce_fusion.1
  1329.0 9.6 convolution_bitcast_fusion.4
  1338.6 8.6 convolution_bitcast_fusion
  1357.9 20.7 multiply_reduce_fusion
  1378.6 22.1 multiply_convert_fusion
  1408.8 8.7 fusion.20
  1417.5 9.6 convolution_bitcast_fusion.5
  1427.2 18.1 fusion.103
  1450.4 6.5 reshape.790
  1474.4 6.5 reshape.787
  1485.2 28.5 reshape.801
  1513.7 27.0 copy.93
  1540.7 12.7 copy.94
  1553.5 19.9 fusion.117
  1617.8 7.6 fusion.115
  1629.2 6.8 constant_dynamic-update-slice_fusion.35
  1636.0 6.4 constant_dynamic-update-slice_fusion.34
  1642.4 9.4 constant_dynamic-update-slice_fusion.33
  1651.8 20.5 constant_dynamic-update-slice_fusion.32
  1672.3 56.0 %broadcast_multiply_fusion = f32[192,280,280]{2,1,0:T(8,128)} fusion(f32[192,280,280]{2,1,0:T(8,128)} %constant_dynamic-update-slice_fusion.32), kind=kLoop, calls=%fused_computation.4 | loop fusion | flops 15052800 | bytes 120422400 | tf_op jit(solution)/shard_map/mul | solution.py:262
  1728.3 56.3 %gather_fusion.1 = f32[192,280,280]{2,1,0:T(8,128)} fusion(f32[192,280,280]{2,1,0:T(8,128)} %broadcast_multiply_fusion, s32[1024]{0:T(1024)} %pad_clamp_fusion), kind=kCustom, calls=%fused_computation.1 | custom fusion | bytes 120423168 | tf_op jit(solution)/shard_map/jit(_take)/gather | solution.py:271
  1784.5 54.2 %broadcast_select_fusion = f32[192,280,280]{2,1,0:T(8,128)} fusion(f32[192,280,280]{2,1,0:T(8,128)} %gather_fusion.1, pred[192]{0:T(512)(128)(4,1)S(1)} %copy-done.79), kind=kLoop, calls=%fused_computation.3 | loop fusion | flops 15052800 | bytes 120422592 | tf_op jit(solution)/shard_map/jit(_take)/select_n | solution.py:271
  1838.8 1137.9 %reduce-scatter.2.cloned.1.call-done = f32[12,280,280]{2,1,0:T(8,128)} async-done(((f32[192,280,280]{2,1,0:T(8,128)}), f32[12,280,280]{2,1,0:T(8,128)}) %reduce-scatter.2.cloned.1.call-update) | async-done | bytes 3763216 | tf_op jit(solution)/shard_map/reduce_scatter | solution.py:272
  2982.9 6.6 copy.96
  2989.6 19.8 fusion.54
  3009.4 39.9 %psum.46 = f32[4,1120]{1,0:T(4,128)S(1)} all-reduce(f32[4,1120]{1,0:T(4,128)S(1)} %maximum_multiply_fusion.1), channel_id=1, replica_groups=mesh['dp'=16,'seq'=2] {'dp','seq'}, use_global_device_ids=true, to_apply=%region_20.21 | all-reduce | flops 4480 | bytes 35840 | tf_op jit(solution)/shard_map/psum | solution.py:258
  3051.3 14.1 fusion.118
  3065.4 17.3 multiply_add_fusion
  3097.7 17.0 multiply_add_fusion.2
  3114.7 14.9 multiply_add_fusion.1
  (361 shorter events, 385.5 us)
Async XLA Ops:
  7.2 768.3 %copy-start.5 = (bf16[1,1024,1120]{1,2,0:T(8,128)(2,1)S(1)}, bf16[1,1024,1120]{1,2,0:T(8,128)(2,1)}, u32[]{:S(2)}) copy-start(bf16[1,1024,1120]{1,2,0:T(8,128)(2,1)} %param.18) | copy-start | bytes 6881284
  7.2 1181.8 %all-reduce.10.cloned.1.call-start = ((), (), s32[]{:S(2)}) async-start(), calls=%async_computation.4 | async-start | bytes 1146880 | tf_op jit(solution)/shard_map/psum | solution.py:26
  7.2 62.5 %collective-permute-start = (bf16[12,280,280]{2,1,0:T(8,128)(2,1)}, bf16[12,280,280]{2,1,0:T(8,128)(2,1)S(1)}, u32[]{:S(2)}, u32[]{:S(2)}) collective-permute-start(bf16[12,280,280]{2,1,0:T(8,128)(2,1)} %param.25), channel_id=1, source_target_pairs={{0,30},{2,0},{4,2},{6,4},{8,6},{10,8},{12,10},{14,12},{16,14},{18,... | collective-permute-start | bytes 5644808 | tf_op jit(solution)/shard_map/ppermute | solution.py:18
  71.3 60.3 %collective-permute-start.1 = (bf16[12,280,280]{2,1,0:T(8,128)(2,1)S(1)}, bf16[12,280,280]{2,1,0:T(8,128)(2,1)S(1)}, u32[]{:S(2)}, u32[]{:S(2)}) collective-permute-start(bf16[12,280,280]{2,1,0:T(8,128)(2,1)S(1)} %collective-permute-done), channel_id=1, source_target_pairs={{0,30},{2,0},{4,2},{6,4},{8,6},{10,8},{12,10},{14,12},{16,14},{18,... | collective-permute-start | bytes 5644808 | tf_op jit(solution)/shard_map/ppermute | solution.py:18
  133.1 59.5 %collective-permute-start.2 = (bf16[12,280,280]{2,1,0:T(8,128)(2,1)S(1)}, bf16[12,280,280]{2,1,0:T(8,128)(2,1)S(1)}, u32[]{:S(2)}, u32[]{:S(2)}) collective-permute-start(bf16[12,280,280]{2,1,0:T(8,128)(2,1)S(1)} %collective-permute-done.1), channel_id=1, source_target_pairs={{0,30},{2,0},{4,2},{6,4},{8,6},{10,8},{12,10},{14,12},{16,14},{18,... | collective-permute-start | bytes 5644808 | tf_op jit(solution)/shard_map/ppermute | solution.py:18
  194.1 58.6 %collective-permute-start.3 = (bf16[12,280,280]{2,1,0:T(8,128)(2,1)S(1)}, bf16[12,280,280]{2,1,0:T(8,128)(2,1)S(1)}, u32[]{:S(2)}, u32[]{:S(2)}) collective-permute-start(bf16[12,280,280]{2,1,0:T(8,128)(2,1)S(1)} %collective-permute-done.2), channel_id=1, source_target_pairs={{0,30},{2,0},{4,2},{6,4},{8,6},{10,8},{12,10},{14,12},{16,14},{18,... | collective-permute-start | bytes 5644808 | tf_op jit(solution)/shard_map/ppermute | solution.py:18
  254.2 57.7 %collective-permute-start.4 = (bf16[12,280,280]{2,1,0:T(8,128)(2,1)S(1)}, bf16[12,280,280]{2,1,0:T(8,128)(2,1)S(1)}, u32[]{:S(2)}, u32[]{:S(2)}) collective-permute-start(bf16[12,280,280]{2,1,0:T(8,128)(2,1)S(1)} %collective-permute-done.3), channel_id=1, source_target_pairs={{0,30},{2,0},{4,2},{6,4},{8,6},{10,8},{12,10},{14,12},{16,14},{18,... | collective-permute-start | bytes 5644808 | tf_op jit(solution)/shard_map/ppermute | solution.py:18
  313.3 56.8 %collective-permute-start.5 = (bf16[12,280,280]{2,1,0:T(8,128)(2,1)S(1)}, bf16[12,280,280]{2,1,0:T(8,128)(2,1)S(1)}, u32[]{:S(2)}, u32[]{:S(2)}) collective-permute-start(bf16[12,280,280]{2,1,0:T(8,128)(2,1)S(1)} %collective-permute-done.4), channel_id=1, source_target_pairs={{0,30},{2,0},{4,2},{6,4},{8,6},{10,8},{12,10},{14,12},{16,14},{18,... | collective-permute-start | bytes 5644808 | tf_op jit(solution)/shard_map/ppermute | solution.py:18
  371.6 55.8 %collective-permute-start.6 = (bf16[12,280,280]{2,1,0:T(8,128)(2,1)S(1)}, bf16[12,280,280]{2,1,0:T(8,128)(2,1)S(1)}, u32[]{:S(2)}, u32[]{:S(2)}) collective-permute-start(bf16[12,280,280]{2,1,0:T(8,128)(2,1)S(1)} %collective-permute-done.5), channel_id=1, source_target_pairs={{0,30},{2,0},{4,2},{6,4},{8,6},{10,8},{12,10},{14,12},{16,14},{18,... | collective-permute-start | bytes 5644808 | tf_op jit(solution)/shard_map/ppermute | solution.py:18
  428.9 54.9 %collective-permute-start.7 = (bf16[12,280,280]{2,1,0:T(8,128)(2,1)S(1)}, bf16[12,280,280]{2,1,0:T(8,128)(2,1)S(1)}, u32[]{:S(2)}, u32[]{:S(2)}) collective-permute-start(bf16[12,280,280]{2,1,0:T(8,128)(2,1)S(1)} %collective-permute-done.6), channel_id=1, source_target_pairs={{0,30},{2,0},{4,2},{6,4},{8,6},{10,8},{12,10},{14,12},{16,14},{18,... | collective-permute-start | bytes 5644808 | tf_op jit(solution)/shard_map/ppermute | solution.py:18
  485.4 54.6 %collective-permute-start.8 = (bf16[12,280,280]{2,1,0:T(8,128)(2,1)S(1)}, bf16[12,280,280]{2,1,0:T(8,128)(2,1)S(1)}, u32[]{:S(2)}, u32[]{:S(2)}) collective-permute-start(bf16[12,280,280]{2,1,0:T(8,128)(2,1)S(1)} %collective-permute-done.7), channel_id=1, source_target_pairs={{0,30},{2,0},{4,2},{6,4},{8,6},{10,8},{12,10},{14,12},{16,14},{18,... | collective-permute-start | bytes 5644808 | tf_op jit(solution)/shard_map/ppermute | solution.py:18
  541.5 54.7 %collective-permute-start.9 = (bf16[12,280,280]{2,1,0:T(8,128)(2,1)S(1)}, bf16[12,280,280]{2,1,0:T(8,128)(2,1)S(1)}, u32[]{:S(2)}, u32[]{:S(2)}) collective-permute-start(bf16[12,280,280]{2,1,0:T(8,128)(2,1)S(1)} %collective-permute-done.8), channel_id=1, source_target_pairs={{0,30},{2,0},{4,2},{6,4},{8,6},{10,8},{12,10},{14,12},{16,14},{18,... | collective-permute-start | bytes 5644808 | tf_op jit(solution)/shard_map/ppermute | solution.py:18
  597.7 55.8 %collective-permute-start.10 = (bf16[12,280,280]{2,1,0:T(8,128)(2,1)S(1)}, bf16[12,280,280]{2,1,0:T(8,128)(2,1)}, u32[]{:S(2)}, u32[]{:S(2)}) collective-permute-start(bf16[12,280,280]{2,1,0:T(8,128)(2,1)S(1)} %collective-permute-done.9), channel_id=1, source_target_pairs={{0,30},{2,0},{4,2},{6,4},{8,6},{10,8},{12,10},{14,12},{16,14},{18,... | collective-permute-start | bytes 5644808 | tf_op jit(solution)/shard_map/ppermute | solution.py:18
  653.5 56.3 %collective-permute-start.11 = (bf16[12,280,280]{2,1,0:T(8,128)(2,1)}, bf16[12,280,280]{2,1,0:T(8,128)(2,1)}, u32[]{:S(2)}, u32[]{:S(2)}) collective-permute-start(bf16[12,280,280]{2,1,0:T(8,128)(2,1)} %collective-permute-done.10), channel_id=1, source_target_pairs={{0,30},{2,0},{4,2},{6,4},{8,6},{10,8},{12,10},{14,12},{16,14},{18,... | collective-permute-start | bytes 5644808 | tf_op jit(solution)/shard_map/ppermute | solution.py:18
  709.8 56.2 %collective-permute-start.12 = (bf16[12,280,280]{2,1,0:T(8,128)(2,1)}, bf16[12,280,280]{2,1,0:T(8,128)(2,1)}, u32[]{:S(2)}, u32[]{:S(2)}) collective-permute-start(bf16[12,280,280]{2,1,0:T(8,128)(2,1)} %collective-permute-done.11), channel_id=1, source_target_pairs={{0,30},{2,0},{4,2},{6,4},{8,6},{10,8},{12,10},{14,12},{16,14},{18,... | collective-permute-start | bytes 5644808 | tf_op jit(solution)/shard_map/ppermute | solution.py:18
  719.6 57.5 %copy-start.73 = (f32[2,1120]{1,0:T(2,128)S(1)}, f32[2,1120]{1,0:T(2,128)}, u32[]{:S(2)}) copy-start(f32[2,1120]{1,0:T(2,128)} %param.23) | copy-start | bytes 26884
  719.6 57.5 %copy-start.74 = (f32[2,1120]{1,0:T(2,128)S(1)}, f32[2,1120]{1,0:T(2,128)}, u32[]{:S(2)}) copy-start(f32[2,1120]{1,0:T(2,128)} %param.22) | copy-start | bytes 26884
  719.6 58.7 %copy-start.13 = (bf16[12,280,280]{2,1,0:T(8,128)(2,1)S(1)}, bf16[12,280,280]{2,1,0:T(8,128)(2,1)}, u32[]{:S(2)}) copy-start(bf16[12,280,280]{2,1,0:T(8,128)(2,1)} %copy-done.12) | copy-start | bytes 5644804
  765.9 56.0 %collective-permute-start.13 = (bf16[12,280,280]{2,1,0:T(8,128)(2,1)}, bf16[12,280,280]{2,1,0:T(8,128)(2,1)S(1)}, u32[]{:S(2)}, u32[]{:S(2)}) collective-permute-start(bf16[12,280,280]{2,1,0:T(8,128)(2,1)} %collective-permute-done.12), channel_id=1, source_target_pairs={{0,30},{2,0},{4,2},{6,4},{8,6},{10,8},{12,10},{14,12},{16,14},{18,... | collective-permute-start | bytes 5644808 | tf_op jit(solution)/shard_map/ppermute | solution.py:18
  775.9 290.5 %copy-start.56 = (f32[1024]{0:T(1024)}, f32[1024]{0:T(1024)S(1)}, u32[]{:S(2)}) copy-start(f32[1024]{0:T(1024)S(1)} %broadcast_multiply_fusion.4) | copy-start | bytes 12292
  777.1 289.2 %copy-start.62 = (f32[1024]{0:T(1024)}, f32[1024]{0:T(1024)S(1)}, u32[]{:S(2)}) copy-start(f32[1024]{0:T(1024)S(1)} %fusion.95) | copy-start | bytes 12292
  778.4 288.0 %copy-start.54 = (f32[1120]{0:T(1024)}, f32[1120]{0:T(1024)S(1)}, u32[]{:S(2)}) copy-start(f32[1120]{0:T(1024)S(1)} %get-tuple-element.94) | copy-start | bytes 13444
  778.4 288.0 %copy-start.64 = (f32[1120]{0:T(1024)}, f32[1120]{0:T(1024)S(1)}, u32[]{:S(2)}) copy-start(f32[1120]{0:T(1024)S(1)} %get-tuple-element.63) | copy-start | bytes 13444
  780.1 48.3 %copy-start.19 = (bf16[12,280,280]{2,1,0:T(8,128)(2,1)S(1)}, bf16[12,280,280]{2,1,0:T(8,128)(2,1)}, u32[]{:S(2)}) copy-start(bf16[12,280,280]{2,1,0:T(8,128)(2,1)} %copy-done.18) | copy-start | bytes 5644804
  781.9 48.3 %copy-start.21 = (bf16[12,280,280]{2,1,0:T(8,128)(2,1)S(1)}, bf16[12,280,280]{2,1,0:T(8,128)(2,1)}, u32[]{:S(2)}) copy-start(bf16[12,280,280]{2,1,0:T(8,128)(2,1)} %copy-done.20) | copy-start | bytes 5644804
  783.6 48.3 %copy-start.23 = (bf16[12,280,280]{2,1,0:T(8,128)(2,1)S(1)}, bf16[12,280,280]{2,1,0:T(8,128)(2,1)}, u32[]{:S(2)}) copy-start(bf16[12,280,280]{2,1,0:T(8,128)(2,1)} %copy-done.22) | copy-start | bytes 5644804
  822.0 49.2 %collective-permute-start.14 = (bf16[12,280,280]{2,1,0:T(8,128)(2,1)S(1)}, bf16[12,280,280]{2,1,0:T(8,128)(2,1)S(1)}, u32[]{:S(2)}, u32[]{:S(2)}) collective-permute-start(bf16[12,280,280]{2,1,0:T(8,128)(2,1)S(1)} %collective-permute-done.13), channel_id=1, source_target_pairs={{0,30},{2,0},{4,2},{6,4},{8,6},{10,8},{12,10},{14,12},{16,14},{18,... | collective-permute-start | bytes 5644808 | tf_op jit(solution)/shard_map/ppermute | solution.py:18
  851.1 21.9 copy-start.11
  1066.3 517.6 %all-reduce.8.cloned.1.call-start = ((), (), s32[]{:S(2)}) async-start(), calls=%async_computation.3 | async-start | bytes 2293760 | tf_op jit(solution)/shard_map/psum | solution.py:229
  1086.0 103.1 %copy-start.2 = (bf16[4,256,20,56]{1,0,3,2:T(4,128)(2,1)}, bf16[4,256,20,56]{1,0,3,2:T(4,128)(2,1)S(1)}, u32[]{:S(2)}) copy-start(bf16[4,256,20,56]{1,0,3,2:T(4,128)(2,1)S(1)} %reshape.769) | copy-start | bytes 6881284
  1189.0 16.6 slice-start
  1189.0 16.6 slice-start.1
  1191.7 21.4 copy-start
  1191.7 14.0 slice-start.2
  1191.8 14.0 slice-start.3
  1191.8 14.7 slice-start.4
  1237.7 77.6 %copy-start.8 = (f32[1024,1120]{0,1:T(8,128)}, f32[1024,1120]{0,1:T(8,128)S(1)}, u32[]{:S(2)}) copy-start(f32[1024,1120]{0,1:T(8,128)S(1)} %get-tuple-element.85) | copy-start | bytes 13762564
  1238.3 26.3 copy-start.34
  1378.6 27.6 copy-start.3
  1408.8 18.3 slice-start.16
  1417.5 27.8 slice-start.18
  1427.2 18.1 slice-start.19
  1456.9 12.4 slice-start.20
  1540.7 12.7 copy-start.35
  1553.4 1423.4 %reduce-scatter.2.cloned.1.call-start = ((), (), s32[]{:S(2)}) async-start(), calls=%async_computation.1 | async-start | bytes 87736320 | tf_op jit(solution)/shard_map/reduce_scatter | solution.py:272
  1553.4 19.9 copy-start.39
  1553.5 19.9 copy-start.44
  1617.8 24.5 slice-start.7
  1617.8 24.5 slice-start.8
  1617.8 24.5 slice-start.9
  1625.5 16.9 slice-start.10
  1629.2 13.2 slice-start.11
  1629.2 13.2 slice-start.12
  1728.3 56.3 %copy-start.79 = (pred[192]{0:T(512)(128)(4,1)S(1)}, pred[192]{0:T(512)(128)(4,1)}, u32[]{:S(2)}) copy-start(pred[192]{0:T(512)(128)(4,1)} %get-tuple-element.96) | copy-start | bytes 580
  1838.7 1212.5 %all-reduce.6.cloned.1.call-start = ((), (), s32[]{:S(2)}) async-start(), calls=%async_computation.2 | async-start | bytes 10321920 | tf_op jit(solution)/shard_map/psum | solution.py:273
  2989.5 19.9 copy-start.68
  2989.5 19.9 copy-start.67
  2989.5 61.1 %copy-start.69 = (f32[1,1120]{1,0:T(1,128)S(1)}, f32[1,1120]{1,0:T(1,128)}, u32[]{:S(2)}) copy-start(f32[1,1120]{1,0:T(1,128)} %get-tuple-element.81) | copy-start | bytes 13444
  2989.5 61.1 %copy-start.70 = (f32[1,1120]{1,0:T(1,128)S(1)}, f32[1,1120]{1,0:T(1,128)}, u32[]{:S(2)}) copy-start(f32[1,1120]{1,0:T(1,128)} %get-tuple-element.83) | copy-start | bytes 13444
  2989.5 61.1 %copy-start.71 = (f32[1,1120]{1,0:T(1,128)S(1)}, f32[1,1120]{1,0:T(1,128)}, u32[]{:S(2)}) copy-start(f32[1,1120]{1,0:T(1,128)} %get-tuple-element.92) | copy-start | bytes 13444
  2989.5 61.1 %copy-start.72 = (f32[1,1120]{1,0:T(1,128)S(1)}, f32[1,1120]{1,0:T(1,128)}, u32[]{:S(2)}) copy-start(f32[1,1120]{1,0:T(1,128)} %get-tuple-element.93) | copy-start | bytes 13444
  3049.3 16.1 copy-start.53
  3091.5 23.2 slice-start.5
  3097.7 17.0 slice-start.6
  (59 other events, 270.8 us)
Sparse Core Ops, SparseCore 0:
  1066.4 20.7 all-reduce.9
  1553.5 21.6 all-reduce.7
  1838.9 1137.8 reduce-scatter.1
  2979.3 28.9 all-reduce.5
